TPU v7x, 256 devices: a whole 4x4x8 slice. The times are simulated.
256 devices in a mesh: row: 4 (over y), col: 32 (over x_lo, z, core), feat: 2 (over x_hi).
Axes of the slice: x: 4 (x_hi: 2, x_lo: 2; x = x_hi * 2 + x_lo), y: 4, z: 8, core: 2. Of those that a mesh axis runs over, the one named last changes fastest.
Arguments:
- panel_student: bfloat16 [2048, 4096], P('row', 'feat'), may hold values from -0.01171875 to 0.01171875
- panel_teacher: bfloat16 [2048, 4096], P('row', 'feat'), may hold values from -0.01171875 to 0.01171875
- tokens_student: bfloat16 [24576, 4096], P('col', 'feat'), may hold values from -0.01171875 to 0.01171875
- tokens_teacher: bfloat16 [24576, 4096], P('col', 'feat'), may hold values from -0.01171875 to 0.01171875
Outputs:
- row_loss: float32 [2048], P(('row', 'col'))
- grad_panel: bfloat16 [2048, 4096], P(('row', 'col'), 'feat')
- grad_tokens: bfloat16 [24576, 4096], P('col', 'feat')
All inputs are finite; a program needn't handle non-finite values.
Results may differ from a plain program's by a relative error of at most 0.0058.
Values may be sent and summed in bfloat16 or wider, within the bound.
No kernel may reach another device: no remote copies, remote signals or barrier semaphores. Data moves between devices by JAX's collectives and lax.ppermute only.
A program may use at most 128 MiB of HBM per device.

v0:
```python
import jax
import jax.numpy as jnp
from jax import lax
from jax.sharding import PartitionSpec as P

epsilon = 1e-06


def squares(features):
    values = features.astype(jnp.float32)
    return jnp.sum(values * values, axis=1)


def inner(left, right):
    return jnp.einsum("rd,cd->rc", left, right, preferred_element_type=jnp.float32)


def inverse(total):
    return 1.0 / jnp.sqrt(total + epsilon)


def local(panel_student, panel_teacher, tokens_student, tokens_teacher):
    student_dots, teacher_dots, sq_ps, sq_pt, sq_ts, sq_tt = lax.psum(
        (
            inner(panel_student, tokens_student),
            inner(panel_teacher, tokens_teacher),
            squares(panel_student),
            squares(panel_teacher),
            squares(tokens_student),
            squares(tokens_teacher),
        ),
        "feat",
    )
    inv_ps = inverse(sq_ps)
    inv_pt = inverse(sq_pt)
    inv_ts = inverse(sq_ts)
    inv_tt = inverse(sq_tt)
    student_gram = student_dots * inv_ps[:, None] * inv_ts[None, :]
    teacher_gram = teacher_dots * inv_pt[:, None] * inv_tt[None, :]
    mismatch = student_gram - teacher_gram
    loss_part = jnp.sum(mismatch * mismatch, axis=1)
    doubled = (2.0 * mismatch).astype(jnp.bfloat16)
    panel_unit = panel_student.astype(jnp.float32) * inv_ps[:, None]
    token_unit = tokens_student.astype(jnp.float32) * inv_ts[:, None]
    panel_half = panel_unit.astype(jnp.bfloat16)
    token_half = token_unit.astype(jnp.bfloat16)
    panel_part = jnp.dot(doubled, token_half, preferred_element_type=jnp.float32)
    panel_term, row_loss = (
        lax.psum_scatter(panel_part, "col", scatter_dimension=0, tiled=True),
        lax.psum_scatter(loss_part, "col", scatter_dimension=0, tiled=True),
    )
    token_part = jnp.einsum("rc,rd->cd", doubled, panel_half, preferred_element_type=jnp.float32)
    token_term = lax.psum(token_part, "row")
    share = panel_student.shape[0] // lax.axis_size("col")
    offset = lax.axis_index("col") * share
    unit_rows = lax.dynamic_slice_in_dim(panel_unit, offset, share, 0)
    inv_rows = lax.dynamic_slice_in_dim(inv_ps, offset, share, 0)
    along_panel, along_tokens = lax.psum(
        (jnp.sum(unit_rows * panel_term, axis=1), jnp.sum(token_unit * token_term, axis=1)), "feat"
    )
    grad_panel = ((panel_term - unit_rows * along_panel[:, None]) * inv_rows[:, None]).astype(
        jnp.bfloat16
    )
    grad_tokens = ((token_term - token_unit * along_tokens[:, None]) * inv_ts[:, None]).astype(
        jnp.bfloat16
    )
    return (row_loss, grad_panel, grad_tokens)


def solution(mesh):
    placed = (P("row", "feat"), P("row", "feat"), P("col", "feat"), P("col", "feat"))
    return jax.shard_map(
        local,
        mesh=mesh,
        in_specs=placed,
        out_specs=(P(("row", "col")), P(("row", "col"), "feat"), P("col", "feat")),
        check_vma=False,
    )
```

profile of v0, /device:TPU:8, one launch (start us, length us, event | category | flops | bytes accessed | tf_op | source)
XLA Modules:
  0.0 405.1 jit_solution(3159031561422616562)
XLA Ops:
  7.2 0.0 copy-start
  7.2 0.0 all-reduce.9.cloned.1.call-start
  7.2 0.0 copy-start.1
  7.2 5.7 %fusion.17 = f32[512,768]{1,0:T(8,128)} fusion(bf16[512,2048]{1,0:T(8,128)(2,1)} %param.5, bf16[768,2048]{1,0:T(8,128)(2,1)} %param.7), kind=kOutput, calls=%fused_computation.31 | convolution fusion | flops 1610612736 | bytes 6815744 | tf_op jit(solution)/shard_map/rd,cd->rc/dot_general | solution.py:15
  12.9 0.0 copy-done
  12.9 0.0 copy-done.1
  12.9 3.1 fusion.16
  15.9 0.0 all-reduce.9.cloned.1.call-update
  16.0 0.0 all-reduce.7.cloned.1.call-start
  16.0 0.0 copy-start.2
  16.0 2.2 multiply_reduce_fusion.1
  18.3 0.0 copy-done.2
  18.3 0.5 fusion.8
  18.7 2.6 multiply_reduce_fusion
  21.3 0.7 fusion.7
  22.0 11.1 %all-reduce.2 = (f32[768]{0:T(1024)S(1)}, f32[512]{0:T(512)S(1)}, f32[768]{0:T(1024)S(1)}, f32[512]{0:T(512)S(1)}) all-reduce(f32[768]{0:T(1024)S(1)} %multiply_reduce_fusion, f32[512]{0:T(512)S(1)} %multiply_reduce_fusion.1, f32[768]{0:T(1024)S(1)} %fusion.7, f32[512]{0:T(512)S(1)} %fusion.8), channel_id=1, replica_groups=mesh['row'=4,'col'=32,'feat'=2] {'feat'}, use_global_device_ids=true, to_apply=%region_9.0 | all-reduce | flops 2560 | bytes 20480 | tf_op jit(solution)/shard_map/psum | solution.py:23
  33.1 85.0 %all-reduce.9.cloned.1.call-done = (f32[512,768]{1,0:T(8,128)}, f32[512,768]{1,0:T(8,128)}) async-done(((f32[512,768]{1,0:T(8,128)}, f32[512,768]{1,0:T(8,128)}), (f32[512,768]{1,0:T(8,128)}, f32[512,768]{1,0:T(8,128)})) %all-reduce.9.cloned.1.call-update) | async-done | bytes 3145744 | tf_op jit(solution)/shard_map/psum | solution.py:23
  118.1 0.0 copy-start.3
  118.1 2.6 multiply_reduce_fusion.2
  120.8 0.0 copy-start.4
  120.8 1.1 copy-done.4
  121.9 0.0 copy-done.3
  121.9 4.6 %fusion.12 = f32[768,2048]{1,0:T(8,128)} fusion(f32[512,768]{1,0:T(8,128)S(1)} %get-tuple-element.12, bf16[512,2048]{1,0:T(8,128)(2,1)S(1)} %copy-done.3, f32[512]{0:T(512)S(1)} %get-tuple-element.16), kind=kOutput, calls=%fused_computation.17 | convolution fusion | flops 1614544896 | bytes 9963520 | tf_op jit(solution)/shard_map/rc,rd->cd/dot_general | solution.py:52
  126.5 0.0 all-reduce.7.cloned.1.call-update
  126.5 0.0 reduce-scatter.2.cloned.1.call-start
  126.6 5.2 %fusion.9 = f32[512,2048]{1,0:T(8,128)} fusion(bf16[768,2048]{1,0:T(8,128)(2,1)S(1)} %copy-done, f32[768]{0:T(1024)S(1)} %get-tuple-element.14, f32[512,768]{1,0:T(8,128)} %copy-done.4), kind=kOutput, calls=%fused_computation.15 | convolution fusion | flops 1616117760 | bytes 8915968 | tf_op jit(solution)/shard_map/dot_general | solution.py:47
  131.8 0.0 copy-start.6
  131.8 0.0 reduce-scatter.2.cloned.1.call-update
  131.9 0.1 dynamic_slice.7
  131.9 0.6 copy-done.6
  132.5 0.6 dynamic-slice
  133.7 4.4 %convert_multiply_fusion.2 = f32[512,2048]{1,0:T(8,128)} fusion(bf16[512,2048]{1,0:T(8,128)(2,1)} %param.4, f32[512]{0:T(512)S(1)} %get-tuple-element.16), kind=kLoop, calls=%fused_computation.11 | loop fusion | flops 2097152 | bytes 6293504 | tf_op jit(solution)/shard_map/mul | solution.py:43
  138.2 55.0 %all-reduce = f32[512]{0:T(512)S(1)} all-reduce(f32[512]{0:T(512)S(1)} %get-tuple-element.11), channel_id=2, replica_groups=mesh['row'=4,'col'=32,'feat'=2] {'col'}, use_global_device_ids=true, to_apply=%region_11.0.clone | all-reduce | flops 512 | bytes 4096
  193.2 0.6 dynamic-slice.1
  193.8 63.3 %all-reduce.7.cloned.1.call-done = f32[768,2048]{1,0:T(8,128)} async-done(((f32[768,2048]{1,0:T(8,128)}), f32[768,2048]{1,0:T(8,128)}) %all-reduce.7.cloned.1.call-update) | async-done | bytes 6291472 | tf_op jit(solution)/shard_map/psum | solution.py:53
  257.1 3.7 fusion.3
  260.9 123.8 %reduce-scatter.2.cloned.1.call-done = f32[16,2048]{1,0:T(8,128)} async-done(((f32[512,2048]{1,0:T(8,128)}), f32[16,2048]{1,0:T(8,128)}) %reduce-scatter.2.cloned.1.call-update) | async-done | bytes 131088 | tf_op jit(solution)/shard_map/reduce_scatter | solution.py:49
  384.7 1.1 multiply_reduce_fusion.3
  385.8 6.5 %all-reduce.1 = (f32[16]{0:T(128)S(1)}, f32[768]{0:T(1024)S(1)}) all-reduce(f32[16]{0:T(128)S(1)} %multiply_reduce_fusion.3, f32[768]{0:T(1024)S(1)} %fusion.3), channel_id=1, replica_groups=mesh['row'=4,'col'=32,'feat'=2] {'feat'}, use_global_device_ids=true, to_apply=%region_14.0 | all-reduce | flops 784 | bytes 6272 | tf_op jit(solution)/shard_map/psum | solution.py:58
  392.3 0.0 copy-start.5
  392.3 4.7 %fusion.6 = bf16[768,2048]{1,0:T(8,128)(2,1)} fusion(f32[768,2048]{1,0:T(8,128)} %all-reduce.7.cloned.1.call-done, bf16[768,2048]{1,0:T(8,128)(2,1)S(1)} %copy-done, f32[768]{0:T(1024)S(1)} %get-tuple-element.4, f32[768]{0:T(1024)S(1)} %get-tuple-element.14), kind=kLoop, calls=%fused_computation.8 | loop fusion | flops 9437184 | bytes 12589056 | tf_op jit(solution)/shard_map/convert_element_type | solution.py:64
  397.0 0.0 copy-done.5
  397.0 1.6 multiply_convert_fusion.3
  (2 shorter events, 0.0 us)
Async XLA Ops:
  7.2 5.7 %copy-start = (bf16[768,2048]{1,0:T(8,128)(2,1)S(1)}, bf16[768,2048]{1,0:T(8,128)(2,1)}, u32[]{:S(2)}) copy-start(bf16[768,2048]{1,0:T(8,128)(2,1)} %param.6) | copy-start | bytes 9437188
  7.2 111.0 %all-reduce.9.cloned.1.call-start = ((), (), s32[]{:S(2)}) async-start(), calls=%async_computation.3 | async-start | bytes 6291456 | tf_op jit(solution)/shard_map/psum | solution.py:23
  7.2 5.7 %copy-start.1 = (bf16[512,2048]{1,0:T(8,128)(2,1)S(1)}, bf16[512,2048]{1,0:T(8,128)(2,1)}, u32[]{:S(2)}) copy-start(bf16[512,2048]{1,0:T(8,128)(2,1)} %param.4) | copy-start | bytes 6291460
  16.0 241.1 %all-reduce.7.cloned.1.call-start = ((), (), s32[]{:S(2)}) async-start(), calls=%async_computation.2 | async-start | bytes 12582912 | tf_op jit(solution)/shard_map/psum | solution.py:53
  16.0 2.2 copy-start.2
  118.1 3.8 copy-start.3
  120.8 1.1 copy-start.4
  126.5 258.1 %reduce-scatter.2.cloned.1.call-start = ((), (), s32[]{:S(2)}) async-start(), calls=%async_computation.1 | async-start | bytes 4325376 | tf_op jit(solution)/shard_map/reduce_scatter | solution.py:49
  131.8 0.7 copy-start.6
  392.3 4.7 %copy-start.5 = (f32[16,2048]{1,0:T(8,128)S(1)}, f32[16,2048]{1,0:T(8,128)}, u32[]{:S(2)}) copy-start(f32[16,2048]{1,0:T(8,128)} %reduce-scatter.2.cloned.1.call-done) | copy-start | bytes 393220
Sparse Core Ops, SparseCore 0:
  16.1 101.9 all-reduce.8
  126.7 130.4 all-reduce.6
  259.7 124.9 reduce-scatter.1
where the time goes:
time: 405 us
  waiting for transfers between devices  272 us (67%)
  blocking collectives  72.6 us (18%)
  other arithmetic  24.2 us (6%)
  matrix products  18.5 us (5%)
  between operations  14.5 us (4%)
    reduce_scatter x1, waiting for transfers between devices, local(): lax.psum_scatter(panel_part, 'col', scatter_dimension=0, tiled=True)  124 us
    psum x1, waiting for transfers between devices, local(): lax.psum((inner(panel_student, tokens_student), inner(panel_teacher, toke...  85 us
    psum x1, waiting for transfers between devices, local(): token_term = lax.psum(token_part, 'row')  63.3 us
    unnamed x1, blocking collectives  55 us
    psum x1, blocking collectives, local(): lax.psum((inner(panel_student, tokens_student), inner(panel_teacher, toke...  11.1 us
    dot_general x2, matrix products, inner(): jnp.einsum('rd,cd->rc', left, right, preferred_element_type=jnp.float32)  8.71 us
  transfers between devices with their start and end apart: 3, of which 3 were waited for; matrix products, arithmetic and copies ran while one was open for 5% of the time, Pallas kernels for 0%

commit v1 on v0

--- a/solution.py
+++ b/solution.py
@@ -50,7 +50,11 @@
         lax.psum_scatter(loss_part, "col", scatter_dimension=0, tiled=True),
     )
     token_part = jnp.einsum("rc,rd->cd", doubled, panel_half, preferred_element_type=jnp.float32)
-    token_term = lax.psum(token_part, "row")
+    token_term = token_part
+    for hop in (1, 2):
+        token_term = token_term + lax.ppermute(
+            token_term, "row", [(dev, dev ^ hop) for dev in range(4)]
+        )
     share = panel_student.shape[0] // lax.axis_size("col")
     offset = lax.axis_index("col") * share
     unit_rows = lax.dynamic_slice_in_dim(panel_unit, offset, share, 0)

time: 405 us -> 438 us (1.081)
  waiting for transfers between devices: 272 us -> 294 us
  other arithmetic: 24.2 us -> 35.5 us
    ppermute x0 -> x2, waiting for transfers between devices: none -> 208 us  [local(): lax.ppermute(token_term, 'row', [(dev, dev ^ hop) for dev in range(4)])]
    reduce_scatter x1, waiting for transfers between devices: 124 us -> 0.01 us  [local(): lax.psum_scatter(panel_part, 'col', scatter_dimension=0, tiled=True)]
    psum x1 -> x0, waiting for transfers between devices: 63.3 us -> none  [local(): token_term = lax.psum(token_part, 'row')]
    add x0 -> x1, other arithmetic: none -> 9.16 us  [local(): token_term + lax.ppermute(token_term, 'row', [(dev, dev ^ hop) for dev in...]
    reduce_sum x1, other arithmetic: 3.74 us -> 8.34 us  [local(): jnp.sum(token_unit * token_term, axis=1)]
  transfers between devices with their start and end apart: 3 -> 4, of which waited for: 3 -> 3; matrix products, arithmetic and copies ran while one was open for 5% -> 5% of each run, Pallas kernels for 0% -> 0%
where the time goes in v1:
time: 438 us
  waiting for transfers between devices  294 us (67%)
  blocking collectives  72 us (16%)
  other arithmetic  35.5 us (8%)
  matrix products  17.2 us (4%)
  between operations  14.8 us (3%)
    ppermute x2, waiting for transfers between devices, local(): lax.ppermute(token_term, 'row', [(dev, dev ^ hop) for dev in range(4)])  208 us
    psum x1, waiting for transfers between devices, local(): lax.psum((inner(panel_student, tokens_student), inner(panel_teacher, toke...  85.9 us
    unnamed x1, blocking collectives  54.4 us
    psum x1, blocking collectives, local(): lax.psum((inner(panel_student, tokens_student), inner(panel_teacher, toke...  11.1 us
    add x1, other arithmetic, local(): token_term + lax.ppermute(token_term, 'row', [(dev, dev ^ hop) for dev in...  9.16 us
  transfers between devices with their start and end apart: 4, of which 3 were waited for; matrix products, arithmetic and copies ran while one was open for 5% of the time, Pallas kernels for 0%

profile of v1, /device:TPU:8, one launch (start us, length us, event | category | flops | bytes accessed | tf_op | source)
XLA Modules:
  0.0 438.0 jit_solution(1045190888579905947)
XLA Ops:
  7.2 0.0 copy-start.2
  7.2 0.0 all-reduce.6.cloned.1.call-start
  7.2 0.0 copy-start.4
  7.2 5.6 %fusion.16 = f32[512,768]{1,0:T(8,128)} fusion(bf16[512,2048]{1,0:T(8,128)(2,1)} %param.4, bf16[768,2048]{1,0:T(8,128)(2,1)} %param.6), kind=kOutput, calls=%fused_computation.30 | convolution fusion | flops 1610612736 | bytes 6815744 | tf_op jit(solution)/shard_map/rd,cd->rc/dot_general | solution.py:15
  12.9 0.0 copy-done.2
  12.9 0.0 copy-done.4
  12.9 3.1 fusion.17
  15.9 0.0 copy-start
  15.9 0.0 all-reduce.6.cloned.1.call-update
  16.0 0.0 reduce-scatter.2.cloned.1.call-start
  16.0 0.0 copy-start.5
  16.0 2.2 fusion.8
  18.3 0.1 copy-done.5
  18.4 0.0 copy-start.3
  18.4 0.5 multiply_reduce_fusion.1
  18.9 0.2 copy-done
  19.1 0.7 fusion.7
  19.8 0.7 copy-done.3
  20.5 0.7 multiply_reduce_fusion
  21.1 11.1 %all-reduce.2 = (f32[768]{0:T(1024)S(1)}, f32[512]{0:T(512)S(1)}, f32[768]{0:T(1024)S(1)}, f32[512]{0:T(512)S(1)}) all-reduce(f32[768]{0:T(1024)S(1)} %multiply_reduce_fusion, f32[512]{0:T(512)S(1)} %multiply_reduce_fusion.1, f32[768]{0:T(1024)S(1)} %fusion.7, f32[512]{0:T(512)S(1)} %fusion.8), channel_id=1, replica_groups=mesh['row'=4,'col'=32,'feat'=2] {'feat'}, use_global_device_ids=true, to_apply=%region_9.0 | all-reduce | flops 2560 | bytes 20480 | tf_op jit(solution)/shard_map/psum | solution.py:23
  32.3 85.9 %all-reduce.6.cloned.1.call-done = (f32[512,768]{1,0:T(8,128)}, f32[512,768]{1,0:T(8,128)}) async-done(((f32[512,768]{1,0:T(8,128)}, f32[512,768]{1,0:T(8,128)}), (f32[512,768]{1,0:T(8,128)}, f32[512,768]{1,0:T(8,128)})) %all-reduce.6.cloned.1.call-update) | async-done | bytes 3145744 | tf_op jit(solution)/shard_map/psum | solution.py:23
  118.2 0.0 copy-start.1
  118.2 2.6 multiply_reduce_fusion.2
  120.8 0.0 copy-done.1
  120.8 4.6 %fusion.12 = f32[768,2048]{1,0:T(8,128)} fusion(f32[512,768]{1,0:T(8,128)S(1)} %get-tuple-element.14, bf16[512,2048]{1,0:T(8,128)(2,1)S(1)} %copy-done.1, f32[512]{0:T(512)S(1)} %get-tuple-element.18), kind=kOutput, calls=%fused_computation.17 | convolution fusion | flops 1614544896 | bytes 9963520 | tf_op jit(solution)/shard_map/rc,rd->cd/dot_general | solution.py:52
  125.4 0.5 collective-permute-start
  125.9 3.9 fusion.9
  129.8 0.0 reduce-scatter.2.cloned.1.call-update
  129.8 0.0 copy-start.7
  129.8 132.9 %collective-permute-done = f32[768,2048]{1,0:T(8,128)} collective-permute-done((f32[768,2048]{1,0:T(8,128)}, f32[768,2048]{1,0:T(8,128)}, u32[]{:S(2)}, u32[]{:S(2)}) %collective-permute-start) | collective-permute-done | bytes 6291488 | tf_op jit(solution)/shard_map/ppermute | solution.py:55
  262.8 9.2 %add.47 = f32[768,2048]{1,0:T(8,128)} add(f32[768,2048]{1,0:T(8,128)} %fusion.12, f32[768,2048]{1,0:T(8,128)} %collective-permute-done) | non-fusion elementwise | flops 1572864 | bytes 18874368 | tf_op jit(solution)/shard_map/add | solution.py:55
  272.0 2.1 collective-permute-start.1
  274.1 0.1 dynamic_slice.7
  274.1 0.0 copy-done.7
  274.1 0.6 dynamic-slice
  275.4 3.9 convert_multiply_fusion.2
  279.2 54.4 %all-reduce = f32[512]{0:T(512)S(1)} all-reduce(f32[512]{0:T(512)S(1)} %get-tuple-element.13), channel_id=2, replica_groups=mesh['row'=4,'col'=32,'feat'=2] {'col'}, use_global_device_ids=true, to_apply=%region_11.0.clone | all-reduce | flops 512 | bytes 4096
  333.7 0.6 dynamic-slice.1
  334.2 0.0 reduce-scatter.2.cloned.1.call-done
  334.3 1.1 multiply_reduce_fusion.3
  335.3 74.7 %collective-permute-done.1 = f32[768,2048]{1,0:T(8,128)} collective-permute-done((f32[768,2048]{1,0:T(8,128)}, f32[768,2048]{1,0:T(8,128)}, u32[]{:S(2)}, u32[]{:S(2)}) %collective-permute-start.1) | collective-permute-done | bytes 6291488 | tf_op jit(solution)/shard_map/ppermute | solution.py:55
  410.0 8.3 %fusion.3 = (f32[768]{0:T(1024)S(1)}, f32[768,2048]{1,0:T(8,128)}) fusion(bf16[768,2048]{1,0:T(8,128)(2,1)S(1)} %copy-done, f32[768]{0:T(1024)S(1)} %get-tuple-element.16, f32[768,2048]{1,0:T(8,128)} %add.47, f32[768,2048]{1,0:T(8,128)} %collective-permute-done.1), kind=kLoop, calls=%fused_computation.5 | loop fusion | flops 7863552 | bytes 22026240 | tf_op jit(solution)/shard_map/reduce_sum | solution.py:63
  418.3 6.5 %all-reduce.1 = (f32[16]{0:T(128)S(1)}, f32[768]{0:T(1024)S(1)}) all-reduce(f32[16]{0:T(128)S(1)} %multiply_reduce_fusion.3, f32[768]{0:T(1024)S(1)} %get-tuple-element.11), channel_id=1, replica_groups=mesh['row'=4,'col'=32,'feat'=2] {'feat'}, use_global_device_ids=true, to_apply=%region_14.0 | all-reduce | flops 784 | bytes 6272 | tf_op jit(solution)/shard_map/psum | solution.py:62
  424.8 0.0 copy-start.6
  424.8 4.7 %fusion.6 = bf16[768,2048]{1,0:T(8,128)(2,1)} fusion(f32[768,2048]{1,0:T(8,128)} %get-tuple-element.12, bf16[768,2048]{1,0:T(8,128)(2,1)S(1)} %copy-done, f32[768]{0:T(1024)S(1)} %get-tuple-element.4, f32[768]{0:T(1024)S(1)} %get-tuple-element.16), kind=kLoop, calls=%fused_computation.8 | loop fusion | flops 9437184 | bytes 12589056 | tf_op jit(solution)/shard_map/convert_element_type | solution.py:68
  429.5 0.0 copy-done.6
  429.5 1.6 multiply_convert_fusion.3
  (2 shorter events, 0.0 us)
Async XLA Ops:
  7.2 5.7 %copy-start.2 = (bf16[768,2048]{1,0:T(8,128)(2,1)S(1)}, bf16[768,2048]{1,0:T(8,128)(2,1)}, u32[]{:S(2)}) copy-start(bf16[768,2048]{1,0:T(8,128)(2,1)} %param.7) | copy-start | bytes 9437188
  7.2 111.0 %all-reduce.6.cloned.1.call-start = ((), (), s32[]{:S(2)}) async-start(), calls=%async_computation.2 | async-start | bytes 6291456 | tf_op jit(solution)/shard_map/psum | solution.py:23
  7.2 5.7 %copy-start.4 = (bf16[512,2048]{1,0:T(8,128)(2,1)S(1)}, bf16[512,2048]{1,0:T(8,128)(2,1)}, u32[]{:S(2)}) copy-start(bf16[512,2048]{1,0:T(8,128)(2,1)} %param.5) | copy-start | bytes 6291460
  15.9 3.2 copy-start
  16.0 318.3 %reduce-scatter.2.cloned.1.call-start = ((), (), s32[]{:S(2)}) async-start(), calls=%async_computation.1 | async-start | bytes 4325376 | tf_op jit(solution)/shard_map/reduce_scatter | solution.py:49
  16.0 2.4 copy-start.5
  18.4 2.1 copy-start.3
  118.2 2.6 copy-start.1
  125.4 137.4 %collective-permute-start = (f32[768,2048]{1,0:T(8,128)}, f32[768,2048]{1,0:T(8,128)}, u32[]{:S(2)}, u32[]{:S(2)}) collective-permute-start(f32[768,2048]{1,0:T(8,128)} %fusion.12), channel_id=1, source_target_pairs={{0,64},{64,0},{128,192},{192,128},{1,65},{65,1},{129,193},{193,129... | collective-permute-start | bytes 18874376 | tf_op jit(solution)/shard_map/ppermute | solution.py:55
  129.8 144.3 %copy-start.7 = (u32[256]{0:T(256)S(1)}, u32[256]{0:T(256)}, u32[]{:S(2)}) copy-start(u32[256]{0:T(256)} %constant.23) | copy-start | bytes 3076
  272.0 138.0 %collective-permute-start.1 = (f32[768,2048]{1,0:T(8,128)}, f32[768,2048]{1,0:T(8,128)}, u32[]{:S(2)}, u32[]{:S(2)}) collective-permute-start(f32[768,2048]{1,0:T(8,128)} %add.47), channel_id=1, source_target_pairs={{0,128},{64,192},{128,0},{192,64},{1,129},{65,193},{129,1},{193,65... | collective-permute-start | bytes 18874376 | tf_op jit(solution)/shard_map/ppermute | solution.py:55
  424.8 4.7 %copy-start.6 = (f32[16,2048]{1,0:T(8,128)S(1)}, f32[16,2048]{1,0:T(8,128)}, u32[]{:S(2)}) copy-start(f32[16,2048]{1,0:T(8,128)} %reduce-scatter.2.cloned.1.call-done) | copy-start | bytes 393220
Sparse Core Ops, SparseCore 0:
  16.1 102.0 all-reduce.5
  130.0 124.1 reduce-scatter.1
